TPU v7x, 256 devices: a whole 4x4x8 slice. The times are simulated.
256 devices in a mesh: section: 32 (over x, z), expert: 8 (over y, core).
Axes of the slice: x: 4, y: 4, z: 8, core: 2. Of those that a mesh axis runs over, the one named last changes fastest.
Arguments:
- tokens: bfloat16 [2048, 4096], P('expert', 'section'), may hold values from -6 to 6
- routes: int32 [2048, 2], P('expert'), may hold values from 0 to 7, all different within a row; in each aligned block of 256 rows (0 to 255, 256 to 511, ...) at most 80 rows name the same one
- mix_weights: float32 [2048, 2], P('expert'), may hold values from 0.2 to 1
- w_gate: bfloat16 [8, 4096, 8192], P('expert', None, 'section'), may hold values from -0.1875 to 0.1875
- w_up: bfloat16 [8, 4096, 8192], P('expert', None, 'section'), may hold values from -0.1875 to 0.1875
- w_down: bfloat16 [8, 8192, 4096], P('expert', 'section'), may hold values from -0.125 to 0.125
- upstream: bfloat16 [2048, 4096], P('expert', 'section'), may hold values from -6 to 6
Outputs:
- mixed: bfloat16 [2048, 4096], P('expert', 'section')
- grad_tokens: bfloat16 [2048, 4096], P('expert', 'section')
- grad_mix: float32 [2048, 2], P('expert')
- grad_gate: bfloat16 [8, 4096, 8192], P('expert', None, 'section')
- grad_up: bfloat16 [8, 4096, 8192], P('expert', None, 'section')
- grad_down: bfloat16 [8, 8192, 4096], P('expert', 'section')
Inputs may be any that keep to these rules, and one draw needn't show every extreme that they name: `routes`: each token names 2 different experts. Among the 256 tokens of one index of the expert axis no expert is named more than 80 times, and in some such block one expert is named exactly 80 times.
All inputs are finite; a program needn't handle non-finite values.
Results may differ from a plain program's by a relative error of at most 0.02.
Values may be sent and summed in bfloat16 or wider, within the bound.
No kernel may reach another device: no remote copies, remote signals or barrier semaphores. Data moves between devices by JAX's collectives and lax.ppermute only.
A program may use at most 128 MiB of HBM per device.

v0:
```python
import jax
import jax.numpy as jnp
from jax import lax
from jax.sharding import PartitionSpec as P

highest = lax.Precision.HIGHEST


def slot_tables(route_rows, mix_rows, capacity, experts):
    tok_count, top_count = route_rows.shape
    flat_routes = route_rows.reshape(-1)
    onehot = (flat_routes[:, None] == jnp.arange(experts, dtype=jnp.int32)[None, :]).astype(
        jnp.int32
    )
    earlier = jnp.cumsum(onehot, axis=0) - onehot
    position = jnp.sum(earlier * onehot, axis=1)
    target = (flat_routes * capacity + position).reshape(tok_count, top_count)
    slot_ids = jnp.arange(experts * capacity, dtype=jnp.int32)
    hits = target[None, :, :] == slot_ids[:, None, None]
    matches = hits.astype(jnp.float32)
    select = jnp.sum(matches, axis=2)
    weighted = jnp.sum(matches * mix_rows[None, :, :], axis=2)
    token_ids = jnp.arange(tok_count, dtype=jnp.int32)
    slot_token = jnp.sum(jnp.sum(hits.astype(jnp.int32), axis=2) * token_ids[None, :], axis=1)
    return (target, select, weighted, slot_token)


def per_device(tokens, routes, mix_weights, w_gate, w_up, w_down, upstream):
    experts = lax.axis_size("expert")
    tok_count = tokens.shape[0]
    top_count = routes.shape[1]
    capacity = 5 * tok_count * top_count // (4 * experts)
    slot_total = experts * capacity
    target, select, weighted, slot_token = slot_tables(routes, mix_weights, capacity, experts)
    slot_fill = jnp.sum(select, axis=1)
    slot_scale = jnp.sum(weighted, axis=1)
    gate_local = w_gate[0]
    up_local = w_up[0]
    down_local = w_down[0]

    def collect(source, factor):
        taken = source[slot_token].astype(jnp.float32)
        return (taken * factor[:, None]).astype(jnp.bfloat16)

    def to_experts(source, factor):
        block = collect(source, factor)
        arrived = lax.all_to_all(
            block.reshape(experts, capacity, -1), "expert", split_axis=0, concat_axis=0, tiled=True
        )
        whole = lax.all_gather(arrived, "section", axis=2, tiled=True)
        return whole.reshape(slot_total, -1)

    def to_sources(partial_value):
        summed = lax.psum_scatter(
            partial_value.reshape(experts, capacity, -1).astype(jnp.bfloat16),
            "section",
            scatter_dimension=2,
            tiled=True,
        )
        back = lax.all_to_all(summed, "expert", split_axis=0, concat_axis=0, tiled=True)
        return back.reshape(slot_total, -1)

    dispatched = to_experts(tokens, slot_fill)
    act_gate = jnp.dot(dispatched, gate_local, preferred_element_type=jnp.float32)
    act_up = jnp.dot(dispatched, up_local, preferred_element_type=jnp.float32)
    sig = jax.nn.sigmoid(act_gate)
    silu_gate = act_gate * sig
    hidden = (silu_gate * act_up).astype(jnp.bfloat16)
    partial_value = jnp.dot(hidden, down_local, preferred_element_type=jnp.float32)
    returned = to_sources(partial_value).astype(jnp.float32)
    moe_out = jnp.dot(weighted.T, returned, precision=highest)
    mixed = (tokens.astype(jnp.float32) + moe_out).astype(jnp.bfloat16)
    picked = returned[target]
    upstream_wide = upstream.astype(jnp.float32)
    mix_terms = jnp.einsum("tkd,td->tk", picked, upstream_wide, precision=highest)
    grad_mix = lax.psum(mix_terms, "section")
    grad_rows = to_experts(upstream, slot_scale)
    grad_hidden = lax.dot_general(
        grad_rows, down_local, (((1,), (1,)), ((), ())), preferred_element_type=jnp.float32
    )
    grad_down = lax.dot_general(
        hidden, grad_rows, (((0,), (0,)), ((), ())), preferred_element_type=jnp.float32
    ).astype(jnp.bfloat16)
    dsilu = sig * (1.0 + act_gate * (1.0 - sig))
    grad_act_gate = (grad_hidden * act_up * dsilu).astype(jnp.bfloat16)
    grad_act_up = (grad_hidden * silu_gate).astype(jnp.bfloat16)
    grad_gate = lax.dot_general(
        dispatched, grad_act_gate, (((0,), (0,)), ((), ())), preferred_element_type=jnp.float32
    ).astype(jnp.bfloat16)
    grad_up = lax.dot_general(
        dispatched, grad_act_up, (((0,), (0,)), ((), ())), preferred_element_type=jnp.float32
    ).astype(jnp.bfloat16)
    first = lax.dot_general(
        grad_act_gate, gate_local, (((1,), (1,)), ((), ())), preferred_element_type=jnp.float32
    )
    second = lax.dot_general(
        grad_act_up, up_local, (((1,), (1,)), ((), ())), preferred_element_type=jnp.float32
    )
    back_rows = to_sources(first + second).astype(jnp.float32)
    grad_moe = jnp.dot(select.T, back_rows, precision=highest)
    grad_tokens = (upstream_wide + grad_moe).astype(jnp.bfloat16)
    return (mixed, grad_tokens, grad_mix, grad_gate[None], grad_up[None], grad_down[None])


def solution(mesh):
    return jax.shard_map(
        per_device,
        mesh=mesh,
        in_specs=(
            P("expert", "section"),
            P("expert", None),
            P("expert", None),
            P("expert", None, "section"),
            P("expert", None, "section"),
            P("expert", "section", None),
            P("expert", "section"),
        ),
        out_specs=(
            P("expert", "section"),
            P("expert", "section"),
            P("expert", None),
            P("expert", None, "section"),
            P("expert", None, "section"),
            P("expert", "section", None),
        ),
        check_vma=False,
    )
```

profile of v0, /device:TPU:8, one launch (start us, length us, event | category | flops | bytes accessed | tf_op | source)
XLA Modules:
  0.0 783.5 jit_solution(15971595313948356913)
XLA Ops:
  7.2 0.0 copy-start
  7.2 0.0 all-gather.3.cloned.1.call-start
  7.3 1.0 copy.30
  8.2 0.1 eq.42
  8.4 0.1 eq.38
  8.5 1.1 reduce-window.6
  9.7 0.2 slice_reduce_fusion
  9.9 0.1 fusion.21
  10.0 0.1 reduce_sum.68
  10.2 0.1 copy.32
  10.2 0.7 compare_select_fusion.1
  10.9 0.3 convert_reduce_fusion.2
  11.2 0.2 multiply_reduce_fusion
  11.4 2.1 select_reduce_fusion
  13.5 0.1 mul.78
  13.6 2.0 gather_fusion
  15.6 0.2 fusion.17
  15.7 10.3 %all_to_all.20 = bf16[8,80,128]{2,1,0:T(8,128)(2,1)} all-to-all(bf16[8,80,128]{2,1,0:T(8,128)(2,1)S(1)} %fusion.17), channel_id=1, replica_groups=mesh['section'=32,'expert'=8] {'expert'}, dimensions={0} | all-to-all | bytes 327680 | tf_op jit(solution)/shard_map/all_to_all | solution.py:47
  26.0 0.0 all-gather.3.cloned.1.call-update
  26.0 0.0 all-gather.5.cloned.1.call-start
  26.1 2.0 gather_fusion.1
  28.1 0.1 mul.83
  28.2 0.2 fusion.16
  28.3 9.5 %all_to_all.21 = bf16[8,80,128]{2,1,0:T(8,128)(2,1)} all-to-all(bf16[8,80,128]{2,1,0:T(8,128)(2,1)S(1)} %fusion.16), channel_id=1, replica_groups=mesh['section'=32,'expert'=8] {'expert'}, dimensions={0} | all-to-all | bytes 327680 | tf_op jit(solution)/shard_map/all_to_all | solution.py:47
  37.9 0.0 all-gather.5.cloned.1.call-update
  37.9 0.0 reduce-scatter.7.cloned.1.call-start
  37.9 77.2 %all-gather.3.cloned.1.call-done = bf16[8,80,4096]{2,1,0:T(8,128)(2,1)} async-done(((bf16[8,80,128]{2,1,0:T(8,128)(2,1)}), bf16[8,80,4096]{2,1,0:T(8,128)(2,1)}) %all-gather.3.cloned.1.call-update) | async-done | bytes 5242896 | tf_op jit(solution)/shard_map/all_gather | solution.py:50
  115.2 5.7 fusion.7
  120.8 2.4 fusion.11
  123.2 81.6 %all-gather.5.cloned.1.call-done = bf16[8,80,4096]{2,1,0:T(8,128)(2,1)} async-done(((bf16[8,80,128]{2,1,0:T(8,128)(2,1)}), bf16[8,80,4096]{2,1,0:T(8,128)(2,1)}) %all-gather.5.cloned.1.call-update) | async-done | bytes 5242896 | tf_op jit(solution)/shard_map/all_gather | solution.py:50
  204.7 5.4 multiply_convert_fusion
  210.1 3.9 convolution_convert_fusion
  214.0 11.2 %copy.36 = bf16[8,80,4096]{1,0,2:T(8,128)(2,1)} copy(bf16[8,80,4096]{2,1,0:T(8,128)(2,1)} %convolution_convert_fusion) | data formatting | bytes 10485760
  225.2 13.1 %reshape.124 = bf16[4096,640]{1,0:T(8,128)(2,1)} reshape(bf16[4096,8,80]{2,1,0:T(8,128)(2,1)} %bitcast.66) | data formatting | bytes 10485760
  238.2 0.0 reduce-scatter.7.cloned.1.call-update
  238.3 0.2 reduce-scatter.9.cloned.1.call-start
  238.5 1.3 copy-done.5
  239.8 2.7 fusion.9
  242.5 3.9 add_convert_fusion
  246.4 11.2 %copy.38 = bf16[8,80,4096]{1,0,2:T(8,128)(2,1)} copy(bf16[8,80,4096]{2,1,0:T(8,128)(2,1)} %bitcast.69) | data formatting | bytes 10485760
  257.6 13.1 %reshape.126 = bf16[4096,640]{1,0:T(8,128)(2,1)} reshape(bf16[4096,8,80]{2,1,0:T(8,128)(2,1)} %bitcast.67) | data formatting | bytes 10485760
  270.7 0.0 reduce-scatter.9.cloned.1.call-update
  270.7 0.1 copy.33
  270.9 0.1 reshape.113
  271.0 0.6 copy-done.9
  271.7 5.7 fusion.1
  277.4 5.8 fusion
  283.2 180.6 %reduce-scatter.7.cloned.1.call-done = bf16[128,640]{1,0:T(8,128)(2,1)} async-done(((bf16[4096,640]{1,0:T(8,128)(2,1)}), bf16[128,640]{1,0:T(8,128)(2,1)}) %reduce-scatter.7.cloned.1.call-update) | async-done | bytes 163856
  463.8 1.2 reshape.125
  465.0 0.8 copy.37
  465.8 4.8 all-to-all-start.1
  470.6 5.8 fusion.2
  476.4 215.3 %reduce-scatter.9.cloned.1.call-done = bf16[128,640]{1,0:T(8,128)(2,1)} async-done(((bf16[4096,640]{1,0:T(8,128)(2,1)}), bf16[128,640]{1,0:T(8,128)(2,1)}) %reduce-scatter.9.cloned.1.call-update) | async-done | bytes 163856
  691.7 1.2 reshape.127
  692.9 0.8 copy.39
  693.7 0.0 all-to-all-done.1
  693.7 4.8 all-to-all-start.3
  698.5 1.3 gather_fusion.2
  699.9 0.4 fusion.18
  700.3 0.1 copy.35
  700.3 72.8 %psum.7 = f32[256,2]{0,1:T(2,128)} all-reduce(f32[256,2]{0,1:T(2,128)S(1)} %bitcast.81), channel_id=1, replica_groups=mesh['section'=32,'expert'=8] {'section'}, use_global_device_ids=true, to_apply=%region_11.12 | all-reduce | flops 512 | bytes 4096 | tf_op jit(solution)/shard_map/psum | solution.py:76
  773.2 2.4 fusion.13
  775.6 0.0 all-to-all-done.3
  775.6 1.4 fusion.14
  (25 shorter events, 0.1 us)
Async XLA Ops:
  7.2 197.6 %copy-start = (bf16[1,256,4096]{2,1,0:T(8,128)(2,1)S(1)}, bf16[1,256,4096]{2,1,0:T(8,128)(2,1)}, u32[]{:S(2)}) copy-start(bf16[1,256,4096]{2,1,0:T(8,128)(2,1)} %param.12) | copy-start | bytes 6291460
  7.2 6.4 copy-start.2
  7.2 18.9 %copy-start.3 = (bf16[256,128]{1,0:T(8,128)(2,1)S(1)}, bf16[256,128]{1,0:T(8,128)(2,1)}, u32[]{:S(2)}) copy-start(bf16[256,128]{1,0:T(8,128)(2,1)} %param.13) | copy-start | bytes 196612
  7.2 108.0 %all-gather.3.cloned.1.call-start = ((), (), s32[]{:S(2)}) async-start(), calls=%async_computation.6 | async-start | bytes 5406720 | tf_op jit(solution)/shard_map/all_gather | solution.py:50
  26.0 178.7 %all-gather.5.cloned.1.call-start = ((), (), s32[]{:S(2)}) async-start(), calls=%async_computation.7 | async-start | bytes 5406720 | tf_op jit(solution)/shard_map/all_gather | solution.py:50
  37.9 425.9 %reduce-scatter.7.cloned.1.call-start = ((), (), s32[]{:S(2)}) async-start(), calls=%async_computation.8 | async-start | bytes 5406720
  115.2 5.7 copy-start.4
  115.2 5.7 copy-start.10
  238.2 1.6 copy-start.5
  238.3 453.4 %reduce-scatter.9.cloned.1.call-start = ((), (), s32[]{:S(2)}) async-start(), calls=%async_computation.9 | async-start | bytes 5406720
  239.8 2.7 copy-start.6
  239.8 2.7 copy-start.8
  270.7 1.0 copy-start.9
  271.7 5.7 copy-start.7
  465.8 227.9 %all-to-all-start.1 = ((bf16[8,80,128]{2,1,0:T(8,128)(2,1)}), bf16[8,80,128]{2,1,0:T(8,128)(2,1)S(1)}, u32[]{:S(2)}, u32[]{:S(2)}) async-start(bf16[8,80,128]{2,1,0:T(8,128)(2,1)} %copy.37), calls=%async_computation.1 | async-start | bytes 327680 | tf_op jit(solution)/shard_map/all_to_all | solution.py:60
  470.6 306.3 %copy-start.1 = (bf16[1,256,4096]{2,1,0:T(8,128)(2,1)S(1)}, bf16[1,256,4096]{2,1,0:T(8,128)(2,1)}, u32[]{:S(2)}) copy-start(bf16[1,256,4096]{2,1,0:T(8,128)(2,1)} %param.12) | copy-start | bytes 6291460
  693.7 81.9 %all-to-all-start.3 = ((bf16[8,80,128]{2,1,0:T(8,128)(2,1)}), bf16[8,80,128]{2,1,0:T(8,128)(2,1)S(1)}, u32[]{:S(2)}, u32[]{:S(2)}) async-start(bf16[8,80,128]{2,1,0:T(8,128)(2,1)} %copy.39), calls=%async_computation.3 | async-start | bytes 327680 | tf_op jit(solution)/shard_map/all_to_all | solution.py:60
Sparse Core Ops, SparseCore 0:
  26.1 88.9 all-gather.2
  117.6 87.0 all-gather.4
  238.4 225.3 reduce-scatter.6
  467.6 224.0 reduce-scatter.8
where the time goes:
time: 785 us; the launch traced here: 783 us
  waiting for transfers between devices  555 us (71%)
  blocking collectives  92.6 us (12%)
  local copies, waits for them, and re-layouts  62.1 us (8%)
  matrix products  45.3 us (6%)
  between operations  14 us (2%)
  starting transfers between devices  9.93 us (1%)
    unnamed x6, waiting for transfers between devices  396 us
    all_gather x2, waiting for transfers between devices, to_experts(): whole = lax.all_gather(arrived, 'section', axis=2, tiled=True)  159 us
    psum x1, blocking collectives, per_device(): grad_mix = lax.psum(mix_terms, 'section')  72.8 us
    unnamed x31, local copies, waits for them, and re-layouts  55.6 us
    all_to_all x2, blocking collectives, to_experts(): lax.all_to_all(block.reshape(experts, capacity, -1), 'expert', split_axis...  19.8 us
  transfers between devices with their start and end apart: 6, of which 4 were waited for; matrix products, arithmetic and copies ran while one was open for 9% of the time, Pallas kernels for 0%

commit v1 on v0

v1 whole, which is shorter than its diff:
```python
import functools

import jax
import jax.numpy as jnp
from jax import lax
from jax.experimental import pallas as pl
from jax.experimental.pallas import tpu as pltpu
from jax.sharding import PartitionSpec as P

highest = lax.Precision.HIGHEST
f32, bf16 = jnp.float32, jnp.bfloat16
NX, NZ = 4, 8
Z_GROUPS = [[x * NZ + z for z in range(NZ)] for x in range(NX)]


def shift_z(value, d):
    pairs = [(x * NZ + z, x * NZ + (z + d) % NZ) for x in range(NX) for z in range(NZ)]
    return lax.ppermute(value, "section", pairs)


def shift_x(value, d):
    pairs = [(x * NZ + z, ((x + d) % NX) * NZ + z) for x in range(NX) for z in range(NZ)]
    return lax.ppermute(value, "section", pairs)


def in_order(relative, own, count):
    held = jnp.stack(relative)
    return jnp.concatenate(
        [lax.dynamic_index_in_dim(held, (own - j) % count, 0, keepdims=False) for j in range(count)],
        axis=1,
    )


def spread_x(value, own):
    parts = value.reshape(value.shape[0], NX, -1).transpose(1, 0, 2)

    def part(d):
        return lax.dynamic_index_in_dim(parts, (own + d) % NX, 0, keepdims=False)

    sent = [shift_x(part(d).astype(bf16), d) for d in range(1, NX)]
    return sum((term.astype(f32) for term in sent), part(0))


def spread_z(value, own):
    parts = value.reshape(value.shape[0], NZ, -1).transpose(1, 0, 2)

    def part(d):
        return lax.dynamic_index_in_dim(parts, (own + d) % NZ, 0, keepdims=False)

    above = shift_z(jnp.stack([part(2), part(3), part(4)]).astype(bf16), 3).astype(f32)
    below = shift_z(jnp.stack([part(-3), part(-2)]).astype(bf16), -3).astype(f32)
    right = shift_z((part(1) + above[2] + below[1]).astype(bf16), 1)
    left = shift_z((part(-1) + above[0]).astype(bf16), -1)
    return part(0) + above[1] + below[0] + right.astype(f32) + left.astype(f32)


def near_z(value):
    return jnp.stack([shift_z(value, 1), value, shift_z(value, -1)])


def far_z(near):
    low, high = shift_z(near, 3), shift_z(near[:2], -3)
    return [low, near, high]


def side_by_side(pieces, own):
    held = jnp.concatenate(pieces)
    return jnp.concatenate(
        [
            lax.dynamic_index_in_dim(held, (j - own + 4) % NZ, 0, keepdims=False)
            for j in range(NZ)
        ],
        axis=1,
    )


def dot_nt(a, b):
    return lax.dot_general(a, b, (((1,), (1,)), ((), ())), preferred_element_type=f32)


def dot_tn(a, b):
    return lax.dot_general(a, b, (((0,), (0,)), ((), ())), preferred_element_type=f32)


def forward_kernel(
    x_ref, tok_ref, gate_ref, up_ref, down_ref, coef_ref, silu_ref, hid_ref, *rest
):
    outs, (acc_gate, acc_up) = rest[:NX], rest[NX:]
    step = pl.program_id(0)
    width = gate_ref.shape[-1]

    @pl.when(step == 0)
    def _():
        acc_gate[...] = jnp.zeros_like(acc_gate)
        acc_up[...] = jnp.zeros_like(acc_up)

    @pl.when(step < NZ)
    def _():
        block = tok_ref[...]
        gate = gate_ref[...].reshape(-1, width)
        up = up_ref[...].reshape(-1, width)
        acc_gate[...] += jnp.dot(block, gate, preferred_element_type=f32)
        acc_up[...] += jnp.dot(block, up, preferred_element_type=f32)

    @pl.when(step == NZ - 1)
    def _():
        act_gate, act_up = acc_gate[...], acc_up[...]
        sig = jax.nn.sigmoid(act_gate)
        silu_gate = act_gate * sig
        silu_ref[...] = silu_gate
        coef_ref[...] = act_up * (sig * (1.0 + act_gate * (1.0 - sig)))
        hid_ref[...] = (silu_gate * act_up).astype(bf16)

    for d in range(NX):

        @pl.when(step == NZ + d)
        def _(d=d):
            outs[d][...] = jnp.dot(
                hid_ref[...], down_ref[...], preferred_element_type=f32
            ).astype(bf16)


def backward_kernel(x_ref, *refs):
    ups = refs[:NX]
    down_ref, gate_ref, up_ref, coef_ref, silu_ref, hid_ref = refs[NX : NX + 6]
    part_ref, gate_out, up_out, mix_out, acc = refs[NX + 6 :]
    step = pl.program_id(0)
    width = gate_ref.shape[-1]

    for d in range(NX):

        @pl.when(step == d)
        def _(d=d):
            term = dot_nt(ups[d][...], down_ref[...])
            acc[...] = term if d == 0 else acc[...] + term

    @pl.when(step == NX - 1)
    def _():
        grad_hidden = acc[...]
        gate_out[...] = (grad_hidden * coef_ref[...]).astype(bf16)
        up_out[...] = (grad_hidden * silu_ref[...]).astype(bf16)
        terms = jnp.sum(grad_hidden * hid_ref[...].astype(f32), axis=1, keepdims=True)
        mix_out[...] = jnp.broadcast_to(terms, mix_out.shape)

    @pl.when(step >= NX)
    def _():
        gate = gate_ref[...].reshape(-1, width)
        up = up_ref[...].reshape(-1, width)
        part_ref[0] = (dot_nt(gate_out[...], gate) + dot_nt(up_out[...], up)).astype(bf16)


def weight_kernel(x_ref, *refs):
    tok_ref, gact_ref, uact_ref, hid_ref = refs[:4]
    ups = refs[4 : 4 + NX]
    gate_out, up_out, down_out = refs[4 + NX :]
    step = pl.program_id(0)

    @pl.when(step < NZ)
    def _():
        block = tok_ref[...]
        gate_out[...] = dot_tn(block, gact_ref[...]).astype(bf16).reshape(gate_out.shape)
        up_out[...] = dot_tn(block, uact_ref[...]).astype(bf16).reshape(up_out.shape)

    for d in range(NX):

        @pl.when(step == NZ + d)
        def _(d=d):
            down_out[...] = dot_tn(hid_ref[...], ups[d][...]).astype(bf16)


def call(kernel, steps, in_specs, out_specs, out_shape, scratch, flops, moved, args):
    return pl.pallas_call(
        kernel,
        grid_spec=pltpu.PrefetchScalarGridSpec(
            num_scalar_prefetch=1,
            grid=(steps,),
            in_specs=in_specs,
            out_specs=out_specs,
            scratch_shapes=scratch,
        ),
        out_shape=out_shape,
        compiler_params=pltpu.CompilerParams(vmem_limit_bytes=50 * 1024 * 1024),
        cost_estimate=pl.CostEstimate(flops=flops, bytes_accessed=moved, transcendentals=0),
    )(*args)


def slot_tables(route_rows, mix_rows, capacity, experts):
    tok_count, top_count = route_rows.shape
    flat_routes = route_rows.reshape(-1)
    onehot = (flat_routes[:, None] == jnp.arange(experts, dtype=jnp.int32)[None, :]).astype(
        jnp.int32
    )
    earlier = jnp.cumsum(onehot, axis=0) - onehot
    position = jnp.sum(earlier * onehot, axis=1)
    target = (flat_routes * capacity + position).reshape(tok_count, top_count)
    slot_ids = jnp.arange(experts * capacity, dtype=jnp.int32)
    hits = target[None, :, :] == slot_ids[:, None, None]
    matches = hits.astype(f32)
    select = jnp.sum(matches, axis=2)
    weighted = jnp.sum(matches * mix_rows[None, :, :], axis=2)
    return (target, select, weighted)


def per_device(tokens, routes, mix_weights, w_gate, w_up, w_down, upstream):
    experts = lax.axis_size("expert")
    section = lax.axis_index("section")
    my_x, my_z = section // NZ, section % NZ
    tok_count, feat = tokens.shape
    top_count = routes.shape[1]
    capacity = 5 * tok_count * top_count // (4 * experts)
    rows = experts * capacity
    ff = w_gate.shape[2]
    wide_x, wide_z = NX * feat, NZ * feat
    full = NX * wide_z
    where = my_x.reshape(1).astype(jnp.int32)
    gate4 = w_gate.reshape(NX, NZ, feat, ff)
    up4 = w_up.reshape(NX, NZ, feat, ff)
    down = w_down[0]

    tok_x = in_order([tokens] + [shift_x(tokens, d) for d in range(1, NX)], my_x, NX)
    tok_x, up_near = lax.optimization_barrier((tok_x, near_z(upstream)))
    up_pieces = far_z(up_near)
    target, select, weighted = slot_tables(routes, mix_weights, capacity, experts)
    slot_scale = jnp.sum(weighted, axis=1)
    select_low = select.astype(bf16)

    def exchange(value):
        return lax.all_to_all(
            value.reshape(experts, capacity, -1), "expert", split_axis=0, concat_axis=0, tiled=True
        ).reshape(rows, -1)

    tok_rows = exchange(jnp.dot(select_low, tok_x, preferred_element_type=f32).astype(bf16))
    tok_rows, up_pieces = lax.optimization_barrier((tok_rows, up_pieces))
    up_z = side_by_side(up_pieces, my_z)
    up_rows = jnp.dot(select_low, up_z, preferred_element_type=f32) * slot_scale[:, None]
    up_rows = exchange(up_rows.astype(bf16))

    dispatched = lax.all_gather(
        tok_rows, "section", axis_index_groups=Z_GROUPS, axis=1, tiled=True
    )
    ups = [up_rows] + [shift_x(up_rows, d) for d in range(1, NX)]

    def whole(*shape):
        return pl.BlockSpec(shape, lambda i, s: (0,) * len(shape))

    def clip(i, low, count):
        return jnp.clip(i - low, 0, count - 1)

    def weight_spec(low):
        return pl.BlockSpec((NX, 1, feat, ff), lambda i, s: (0, clip(i, low, NZ), 0, 0))

    def struct(shape, kind):
        return jax.ShapeDtypeStruct(shape, kind)

    tok_spec = pl.BlockSpec((rows, wide_x), lambda i, s: (0, clip(i, 0, NZ)))
    coef, silu_gate, hidden, *outs = call(
        forward_kernel,
        NZ + NX,
        [
            tok_spec,
            weight_spec(0),
            weight_spec(0),
            pl.BlockSpec((ff, wide_z), lambda i, s: (0, (s[0] + clip(i, NZ, NX)) % NX)),
        ],
        [whole(rows, ff)] * 3 + [whole(rows, wide_z)] * NX,
        [struct((rows, ff), f32)] * 2
        + [struct((rows, ff), bf16)]
        + [struct((rows, wide_z), bf16)] * NX,
        [pltpu.VMEM((rows, ff), f32)] * 2,
        6 * rows * full * ff,
        2 * (2 * rows * full + 3 * full * ff),
        (where, dispatched, gate4, up4, down),
    )

    sent_x = [shift_x(outs[d], d) for d in range(1, NX)]

    back, gate_act, up_act, mix_part = call(
        backward_kernel,
        NX + NZ,
        [whole(rows, wide_z)] * NX
        + [
            pl.BlockSpec((ff, wide_z), lambda i, s: (0, (s[0] + NX - clip(i, 0, NX)) % NX)),
            weight_spec(NX),
            weight_spec(NX),
        ]
        + [whole(rows, ff)] * 3,
        [pl.BlockSpec((1, rows, wide_x), lambda i, s: (clip(i, NX, NZ), 0, 0))]
        + [whole(rows, ff)] * 2
        + [whole(rows, 128)],
        [struct((NZ, rows, wide_x), bf16)]
        + [struct((rows, ff), bf16)] * 2
        + [struct((rows, 128), f32)],
        [pltpu.VMEM((rows, ff), f32)],
        0,
        0,
        (where, *ups, down, gate4, up4, coef, silu_gate, hidden),
    )

    back_z = lax.psum_scatter(
        back.reshape(NZ * rows, wide_x),
        "section",
        axis_index_groups=Z_GROUPS,
        scatter_dimension=0,
        tiled=True,
    )
    grad_gate, grad_up, grad_down = call(
        weight_kernel,
        NZ + NX,
        [tok_spec] + [whole(rows, ff)] * 3 + [whole(rows, wide_z)] * NX,
        [weight_spec(0)] * 2
        + [pl.BlockSpec((ff, wide_z), lambda i, s: (0, (s[0] + NX - clip(i, NZ, NX)) % NX))],
        [struct((NX, NZ, feat, ff), bf16)] * 2 + [struct((ff, full), bf16)],
        [],
        0,
        0,
        (where, dispatched, gate_act, up_act, hidden, *ups),
    )

    mix_sum = mix_part[:, 0].reshape(experts, capacity)

    sent_x, grads, mix_sum = lax.optimization_barrier(
        (sent_x, (grad_gate, grad_up, grad_down), mix_sum)
    )
    grad_gate, grad_up, grad_down = grads

    summed = outs[0].astype(f32)
    for term in sent_x:
        summed = summed + term.astype(f32)
    summed, mix_sum = lax.optimization_barrier((summed.astype(bf16), mix_sum))
    returned = exchange(summed).astype(f32)
    moe_out = jnp.dot(weighted.T, returned, precision=highest)
    mixed = (tokens.astype(f32) + spread_z(moe_out, my_z)).astype(bf16)

    for d in (2, 1):
        mix_sum = mix_sum + shift_x(mix_sum, d)
    for d in (4, 2, 1):
        mix_sum = mix_sum + shift_z(mix_sum, d)
    mix_rows = lax.all_to_all(mix_sum, "expert", split_axis=0, concat_axis=0, tiled=True)
    grad_mix = mix_rows.reshape(-1)[target] / mix_weights

    back_rows = exchange(back_z).astype(f32)
    grad_moe = jnp.dot(select.T, back_rows, precision=highest)
    grad_tokens = (upstream.astype(f32) + spread_x(grad_moe, my_x)).astype(bf16)
    return (
        mixed,
        grad_tokens,
        grad_mix,
        grad_gate.reshape(1, full, ff),
        grad_up.reshape(1, full, ff),
        grad_down[None],
    )


def solution(mesh):
    return jax.shard_map(
        per_device,
        mesh=mesh,
        in_specs=(
            P("expert", "section"),
            P("expert", None),
            P("expert", None),
            P("expert", None, "section"),
            P("expert", None, "section"),
            P("expert", "section", None),
            P("expert", "section"),
        ),
        out_specs=(
            P("expert", "section"),
            P("expert", "section"),
            P("expert", None),
            P("expert", None, "section"),
            P("expert", None, "section"),
            P("expert", "section", None),
        ),
        check_vma=False,
    )
```

time: 785 us -> 299 us (0.38)
  waiting for transfers between devices: 555 us -> 122 us
  blocking collectives: 92.6 us -> 22.1 us
  starting transfers between devices: 9.93 us -> 66 us
  local copies, waits for them, and re-layouts: 62.1 us -> 14.3 us
  Pallas kernels: 0 us -> 40.3 us
  matrix products: 45.3 us -> 5.32 us
  other arithmetic: 4.84 us -> 13.1 us
    unnamed x6 -> x2, waiting for transfers between devices: 396 us -> 0.03 us
    all_gather x2 -> x1, waiting for transfers between devices: 159 us -> 38 us  [per_device(): lax.all_gather(tok_rows, 'section', axis_index_groups=Z_GROUPS, axis=1, t...]
    ppermute x0 -> x25, waiting for transfers between devices: none -> 84.3 us  [the longest x14 56.7 us: shift_x(): return lax.ppermute(value, 'section', pairs)]
    psum x1 -> x0, blocking collectives: 72.8 us -> none  [per_device(): grad_mix = lax.psum(mix_terms, 'section')]
    unnamed x31 -> x42, local copies, waits for them, and re-layouts: 55.6 us -> 7.86 us
    ppermute x0 -> x25, starting transfers between devices: none -> 46.8 us  [the longest x11 29.5 us: shift_z(): return lax.ppermute(value, 'section', pairs)]
    pallas_call x0 -> x3, Pallas kernels: none -> 40.3 us  [call(): pl.pallas_call(kernel, grid_spec=pltpu.PrefetchScalarGridSpec(num_scalar_...]
    dot_general x10 -> x2, matrix products: 41.5 us -> 1.69 us  [the longest x1 1.17 us: per_device(): jnp.dot(select_low, tok_x, preferred_element_type=f32).astype(bf16)]
  transfers between devices with their start and end apart: 6 -> 31, of which waited for: 4 -> 16; matrix products, arithmetic and copies ran while one was open for 9% -> 8% of each run, Pallas kernels for 0% -> 9%
where the time goes in v1:
time: 299 us; the launch traced here: 298 us
  waiting for transfers between devices  122 us (41%)
  starting transfers between devices  66 us (22%)
  Pallas kernels  40.3 us (13%)
  blocking collectives  22.1 us (7%)
  between operations  14.8 us (5%)
  local copies, waits for them, and re-layouts  14.3 us (5%)
  other arithmetic  13.1 us (4%)
  matrix products  5.32 us (2%)
    ppermute x14, waiting for transfers between devices, shift_x(): return lax.ppermute(value, 'section', pairs)  56.7 us
    pallas_call x3, Pallas kernels, call(): pl.pallas_call(kernel, grid_spec=pltpu.PrefetchScalarGridSpec(num_scalar_...  40.3 us
    all_gather x1, waiting for transfers between devices, per_device(): lax.all_gather(tok_rows, 'section', axis_index_groups=Z_GROUPS, axis=1, t...  38 us
    ppermute x11, starting transfers between devices, shift_z(): return lax.ppermute(value, 'section', pairs)  29.5 us
    ppermute x11, waiting for transfers between devices, shift_z(): return lax.ppermute(value, 'section', pairs)  27.5 us
    all_to_all x1, blocking collectives, exchange(): lax.all_to_all(value.reshape(experts, capacity, -1), 'expert', split_axis...  22.1 us
    ppermute x14, starting transfers between devices, shift_x(): return lax.ppermute(value, 'section', pairs)  17.3 us
    all_to_all x3, starting transfers between devices, exchange(): lax.all_to_all(value.reshape(experts, capacity, -1), 'expert', split_axis...  14.3 us
  transfers between devices with their start and end apart: 31, of which 16 were waited for; matrix products, arithmetic and copies ran while one was open for 8% of the time, Pallas kernels for 9%

profile of v1, /device:TPU:8, one launch (start us, length us, event | category | flops | bytes accessed | tf_op | source)
XLA Modules:
  0.0 298.1 jit_solution(2590715519264180082)
XLA Ops:
  7.2 1.6 collective-permute-start
  8.8 2.7 collective-permute-start.1
  11.5 1.4 collective-permute-start.2
  12.9 1.9 collective-permute-start.3
  14.8 3.9 %collective-permute-start.4 = (bf16[256,128]{1,0:T(8,128)(2,1)}, bf16[256,128]{1,0:T(8,128)(2,1)S(1)}, u32[]{:S(2)}, u32[]{:S(2)}) collective-permute-start(bf16[256,128]{1,0:T(8,128)(2,1)} %param.13), channel_id=1, source_target_pairs={{0,56},{8,0},{16,8},{24,16},{32,24},{40,32},{48,40},{56,48},{64,12... | collective-permute-start | bytes 196616 | tf_op jit(solution)/shard_map/ppermute | solution.py:18
  18.8 0.8 copy.48
  19.9 1.1 reduce-window.6
  21.6 0.7 compare_select_fusion
  22.3 2.0 select_reduce_fusion.1
  24.5 1.2 convolution_convert_fusion
  25.7 4.9 %all-to-all-start = ((bf16[8,80,512]{2,1,0:T(8,128)(2,1)}), bf16[8,80,512]{2,1,0:T(8,128)(2,1)S(1)}, u32[]{:S(2)}, u32[]{:S(2)}) async-start(bf16[8,80,512]{2,1,0:T(8,128)(2,1)} %bitcast.15), calls=%async_computation | async-start | bytes 1310720 | tf_op jit(solution)/shard_map/all_to_all | solution.py:228
  30.6 2.1 collective-permute-start.5
  32.7 3.1 %collective-permute-start.6 = (bf16[2,256,128]{2,1,0:T(8,128)(2,1)S(1)}, bf16[2,256,128]{2,1,0:T(8,128)(2,1)S(1)}, u32[]{:S(2)}, u32[]{:S(2)}) collective-permute-start(bf16[2,256,128]{2,1,0:T(8,128)(2,1)S(1)} %slice.29), channel_id=1, source_target_pairs={{0,40},{8,48},{16,56},{24,0},{32,8},{40,16},{48,24},{56,32},{64,10... | collective-permute-start | bytes 393224 | tf_op jit(solution)/shard_map/ppermute | solution.py:18
  35.7 4.3 %collective-permute-done.6 = bf16[2,256,128]{2,1,0:T(8,128)(2,1)S(1)} collective-permute-done((bf16[2,256,128]{2,1,0:T(8,128)(2,1)S(1)}, bf16[2,256,128]{2,1,0:T(8,128)(2,1)S(1)}, u32[]{:S(2)}, u32[]{:S(2)}) %collective-permute-start.6) | collective-permute-done | bytes 131104 | tf_op jit(solution)/shard_map/ppermute | solution.py:18
  40.0 6.5 %collective-permute-done.5 = bf16[3,256,128]{2,1,0:T(8,128)(2,1)S(1)} collective-permute-done((bf16[3,256,128]{2,1,0:T(8,128)(2,1)S(1)}, bf16[3,256,128]{2,1,0:T(8,128)(2,1)S(1)}, u32[]{:S(2)}, u32[]{:S(2)}) %collective-permute-start.5) | collective-permute-done | bytes 196640 | tf_op jit(solution)/shard_map/ppermute | solution.py:18
  46.5 0.8 copy-done.11
  48.4 22.1 %all_to_all.29 = bf16[8,80,1024]{2,1,0:T(8,128)(2,1)S(1)} all-to-all(bf16[8,80,1024]{2,1,0:T(8,128)(2,1)S(1)} %bitcast.150), channel_id=1, replica_groups=mesh['section'=32,'expert'=8] {'expert'}, dimensions={0} | all-to-all | bytes 2621440 | tf_op jit(solution)/shard_map/all_to_all | solution.py:228
  71.1 0.9 collective-permute-start.11
  72.0 1.8 collective-permute-start.12
  73.8 38.0 %all-gather.2.cloned.1.call-done.tok_ref.refs_0_ = bf16[640,4096]{1,0:T(8,128)(2,1)} async-done(((bf16[640,512]{1,0:T(8,128)(2,1)}), bf16[640,4096]{1,0:T(8,128)(2,1)}) %all-gather.2.cloned.1.call-update) | async-done | bytes 5242896 | tf_op jit(solution)/shard_map/all_gather | solution.py:238
  111.8 13.8 %shard_map.118 = (f32[640,256]{1,0:T(8,128)S(1)}, f32[640,256]{1,0:T(8,128)S(1)}, bf16[640,256]{1,0:T(8,128)(2,1)S(1)}, bf16[640,1024]{1,0:T(8,128)(2,1)S(1)}, b...) custom-call(s32[1]{0:T(128)} %bitcast.3.x_ref, ...), custom_call_target="tpu_custom_call" | custom-call | flops 4026531840 | bytes 16777216 | tf_op jit(solution)/shard_map/pallas_call | solution.py:172
  125.6 1.1 copy-done.2
  126.7 3.7 %collective-permute-done.10.refs_1_.refs_5_ = bf16[640,1024]{1,0:T(8,128)(2,1)S(1)} collective-permute-done((bf16[640,1024]{1,0:T(8,128)(2,1)S(1)}, bf16[640,1024]{1,0:T(8,128)(2,1)S(1)}, u32[]{:S(2)}, u32[]{:S(2)}) %collective-permute-start.10) | collective-permute-done | bytes 1310752 | tf_op jit(solution)/shard_map/ppermute | solution.py:23
  130.4 0.7 collective-permute-done.12.refs_3_.refs_7_
  131.4 13.5 %shard_map.119 = (bf16[8,640,512]{2,1,0:T(8,128)(2,1)}, bf16[640,256]{1,0:T(8,128)(2,1)S(1)}, bf16[640,256]{1,0:T(8,128)(2,1)S(1)}, f32[640,128]{1,0:T(8,128)S(1)}) custom-call(s32[1]{0:T(128)} %bitcast.3.x_ref, bf16[640,1024]{1,0:T(8,128)(2,1)S(1)} %bitcast.145, bf16[640,1024]{1,0:T(8,128)(2,1)} %copy-done, ...), custom_call_target="tpu_custom_call" | custom-call | tf_op jit(solution)/shard_map/pallas_call | solution.py:172
  144.9 0.7 copy-done.4
  145.6 0.7 copy-done.6
  146.5 3.5 %collective-permute-start.8 = (bf16[640,1024]{1,0:T(8,128)(2,1)}, bf16[640,1024]{1,0:T(8,128)(2,1)}, u32[]{:S(2)}, u32[]{:S(2)}) collective-permute-start(bf16[640,1024]{1,0:T(8,128)(2,1)} %get-tuple-element.40), channel_id=1, source_target_pairs={{0,128},{8,136},{16,144},{24,152},{32,160},{40,168},{48,176},{56,1... | collective-permute-start | bytes 3932168 | tf_op jit(solution)/shard_map/ppermute | solution.py:23
  150.0 1.1 slice_reduce_fusion
  151.2 1.0 copy-done.5
  152.2 13.0 %shard_map.120 = (bf16[4,8,128,256]{3,2,1,0:T(8,128)(2,1)}, bf16[4,8,128,256]{3,2,1,0:T(8,128)(2,1)}, bf16[256,4096]{1,0:T(8,128)(2,1)}) custom-call(s32[1]{0:T(128)} %bitcast.3.x_ref, bf16[640,4096]{1,0:T(8,128)(2,1)} %all-gather.2.cloned.1.call-done.tok_ref.refs_0_, bf16[640,256]{1,0:T(8,128)(2,1)S(1)} %get-tuple-element.48.refs_1_, ...), custom_call_target="tpu_custom_call" | custom-call | tf_op jit(solution)/shard_map/pallas_call | solution.py:172
  165.2 12.8 %collective-permute-done.7 = bf16[640,1024]{1,0:T(8,128)(2,1)} collective-permute-done((bf16[640,1024]{1,0:T(8,128)(2,1)}, bf16[640,1024]{1,0:T(8,128)(2,1)}, u32[]{:S(2)}, u32[]{:S(2)}) %collective-permute-start.7) | collective-permute-done | bytes 1310752 | tf_op jit(solution)/shard_map/ppermute | solution.py:23
  178.0 28.8 %collective-permute-done.8 = bf16[640,1024]{1,0:T(8,128)(2,1)} collective-permute-done((bf16[640,1024]{1,0:T(8,128)(2,1)}, bf16[640,1024]{1,0:T(8,128)(2,1)}, u32[]{:S(2)}, u32[]{:S(2)}) %collective-permute-start.8) | collective-permute-done | bytes 1310752 | tf_op jit(solution)/shard_map/ppermute | solution.py:23
  206.8 4.4 %add_convert_fusion = bf16[640,1024]{1,0:T(8,128)(2,1)} fusion(bf16[640,1024]{1,0:T(8,128)(2,1)} %collective-permute-done.9, bf16[640,1024]{1,0:T(8,128)(2,1)} %collective-permute-done.8, bf16[640,1024]{1,0:T(8,128)(2,1)} %collective-permute-done.7, bf16[640,1024]{1,0:T(8,128)(2,1)S(1)} %copy-done.3), kind=kLoop, calls=%fused_computation.1 | loop fusion | flops 5242880 | bytes 6553600 | tf_op jit(solution)/shard_map/convert_element_type | solution.py:329
  211.1 4.6 %all-to-all-start.2 = ((bf16[8,80,1024]{2,1,0:T(8,128)(2,1)}), bf16[8,80,1024]{2,1,0:T(8,128)(2,1)S(1)}, u32[]{:S(2)}, u32[]{:S(2)}) async-start(bf16[8,80,1024]{2,1,0:T(8,128)(2,1)} %bitcast.30), calls=%async_computation.2 | async-start | bytes 2621440 | tf_op jit(solution)/shard_map/all_to_all | solution.py:228
  215.7 1.0 collective-permute-start.20
  216.7 4.1 %collective-permute-done.20 = f32[8,80]{1,0:T(8,128)S(1)} collective-permute-done((f32[8,80]{1,0:T(8,128)S(1)}, f32[8,80]{1,0:T(8,128)S(1)}, u32[]{:S(2)}, u32[]{:S(2)}) %collective-permute-start.20) | collective-permute-done | bytes 2592 | tf_op jit(solution)/shard_map/ppermute | solution.py:23
  221.2 4.5 %collective-permute-done.21 = f32[8,80]{1,0:T(8,128)S(1)} collective-permute-done((f32[8,80]{1,0:T(8,128)S(1)}, f32[8,80]{1,0:T(8,128)S(1)}, u32[]{:S(2)}, u32[]{:S(2)}) %collective-permute-start.21) | collective-permute-done | bytes 2592 | tf_op jit(solution)/shard_map/ppermute | solution.py:23
  225.6 6.5 %collective-permute-start.22 = (f32[8,80]{1,0:T(8,128)S(1)}, f32[8,80]{1,0:T(8,128)S(1)}, u32[]{:S(2)}, u32[]{:S(2)}) collective-permute-start(f32[8,80]{1,0:T(8,128)S(1)} %add.370), channel_id=1, source_target_pairs={{0,32},{8,40},{16,48},{24,56},{32,0},{40,8},{48,16},{56,24},{64,96... | collective-permute-start | bytes 7688 | tf_op jit(solution)/shard_map/ppermute | solution.py:18
  232.1 1.6 collective-permute-done.22
  233.7 1.0 collective-permute-start.23
  234.8 4.7 %collective-permute-done.23 = f32[8,80]{1,0:T(8,128)S(1)} collective-permute-done((f32[8,80]{1,0:T(8,128)S(1)}, f32[8,80]{1,0:T(8,128)S(1)}, u32[]{:S(2)}, u32[]{:S(2)}) %collective-permute-start.23) | collective-permute-done | bytes 2592 | tf_op jit(solution)/shard_map/ppermute | solution.py:18
  239.5 2.5 collective-permute-start.24
  242.0 2.3 collective-permute-done.24
  244.9 4.8 %all-to-all-start.4 = ((f32[8,1,80]{2,1,0:T(1,128)}), f32[8,1,80]{2,1,0:T(1,128)S(1)}, u32[]{:S(2)}, u32[]{:S(2)}) async-start(f32[8,1,80]{2,1,0:T(1,128)} %bitcast.58), calls=%async_computation.5 | async-start | bytes 8192 | tf_op jit(solution)/shard_map/all_to_all | solution.py:338
  249.7 0.7 copy.51
  250.8 2.4 fusion.2
  253.2 1.0 copy-done.9
  254.2 4.8 %all-to-all-start.3 = ((bf16[8,80,512]{2,1,0:T(8,128)(2,1)}), bf16[8,80,512]{2,1,0:T(8,128)(2,1)S(1)}, u32[]{:S(2)}, u32[]{:S(2)}) async-start(bf16[8,80,512]{2,1,0:T(8,128)(2,1)} %bitcast.160), calls=%async_computation.4 | async-start | bytes 1310720 | tf_op jit(solution)/shard_map/all_to_all | solution.py:228
  259.1 3.1 %collective-permute-start.13 = (bf16[3,256,128]{2,1,0:T(8,128)(2,1)S(1)}, bf16[3,256,128]{2,1,0:T(8,128)(2,1)S(1)}, u32[]{:S(2)}, u32[]{:S(2)}) collective-permute-start(bf16[3,256,128]{2,1,0:T(8,128)(2,1)S(1)} %pad_maximum_fusion.3), channel_id=1, source_target_pairs={{0,24},{8,32},{16,40},{24,48},{32,56},{40,0},{48,8},{56,16},{64,88... | collective-permute-start | bytes 589832 | tf_op jit(solution)/shard_map/ppermute | solution.py:18
  262.2 2.1 collective-permute-start.14
  265.4 0.7 reduce.8
  266.1 2.3 gather_fusion
  268.6 0.7 copy.58
  269.6 7.9 %collective-permute-done.13 = bf16[3,256,128]{2,1,0:T(8,128)(2,1)S(1)} collective-permute-done((bf16[3,256,128]{2,1,0:T(8,128)(2,1)S(1)}, bf16[3,256,128]{2,1,0:T(8,128)(2,1)S(1)}, u32[]{:S(2)}, u32[]{:S(2)}) %collective-permute-start.13) | collective-permute-done | bytes 196640 | tf_op jit(solution)/shard_map/ppermute | solution.py:18
  277.5 1.0 fusion.9
  278.9 2.9 collective-permute-start.16
  282.2 1.3 fusion
  283.6 2.4 collective-permute-start.18
  286.0 0.8 collective-permute-start.19
  286.8 1.6 fusion.15
  288.4 1.3 collective-permute-done.17
  289.8 0.9 collective-permute-done.19
  290.6 0.7 fusion.20
  (97 shorter events, 6.7 us)
Async XLA Ops:
  7.2 17.2 %copy-start.12 = (bf16[256,128]{1,0:T(8,128)(2,1)S(1)}, bf16[256,128]{1,0:T(8,128)(2,1)}, u32[]{:S(2)}) copy-start(bf16[256,128]{1,0:T(8,128)(2,1)} %param.7) | copy-start | bytes 196612
  7.2 17.1 %copy-start.13 = (bf16[256,128]{1,0:T(8,128)(2,1)S(1)}, bf16[256,128]{1,0:T(8,128)(2,1)}, u32[]{:S(2)}) copy-start(bf16[256,128]{1,0:T(8,128)(2,1)} %param.13) | copy-start | bytes 196612
  7.2 17.2 %collective-permute-start = (bf16[256,128]{1,0:T(8,128)(2,1)}, bf16[256,128]{1,0:T(8,128)(2,1)S(1)}, u32[]{:S(2)}, u32[]{:S(2)}) collective-permute-start(bf16[256,128]{1,0:T(8,128)(2,1)} %param.7), channel_id=1, source_target_pairs={{0,64},{8,72},{16,80},{24,88},{32,96},{40,104},{48,112},{56,120},{... | collective-permute-start | bytes 196616 | tf_op jit(solution)/shard_map/ppermute | solution.py:23
  8.8 15.6 %collective-permute-start.1 = (bf16[256,128]{1,0:T(8,128)(2,1)}, bf16[256,128]{1,0:T(8,128)(2,1)S(1)}, u32[]{:S(2)}, u32[]{:S(2)}) collective-permute-start(bf16[256,128]{1,0:T(8,128)(2,1)} %param.7), channel_id=1, source_target_pairs={{0,128},{8,136},{16,144},{24,152},{32,160},{40,168},{48,176},{56,1... | collective-permute-start | bytes 196616 | tf_op jit(solution)/shard_map/ppermute | solution.py:23
  11.5 12.9 %collective-permute-start.2 = (bf16[256,128]{1,0:T(8,128)(2,1)}, bf16[256,128]{1,0:T(8,128)(2,1)S(1)}, u32[]{:S(2)}, u32[]{:S(2)}) collective-permute-start(bf16[256,128]{1,0:T(8,128)(2,1)} %param.7), channel_id=1, source_target_pairs={{0,192},{8,200},{16,208},{24,216},{32,224},{40,232},{48,240},{56,2... | collective-permute-start | bytes 196616 | tf_op jit(solution)/shard_map/ppermute | solution.py:23
  12.9 11.4 %collective-permute-start.3 = (bf16[256,128]{1,0:T(8,128)(2,1)}, bf16[256,128]{1,0:T(8,128)(2,1)S(1)}, u32[]{:S(2)}, u32[]{:S(2)}) collective-permute-start(bf16[256,128]{1,0:T(8,128)(2,1)} %param.13), channel_id=1, source_target_pairs={{0,8},{8,16},{16,24},{24,32},{32,40},{40,48},{48,56},{56,0},{64,72... | collective-permute-start | bytes 196616 | tf_op jit(solution)/shard_map/ppermute | solution.py:18
  14.8 9.5 %collective-permute-start.4 = (bf16[256,128]{1,0:T(8,128)(2,1)}, bf16[256,128]{1,0:T(8,128)(2,1)S(1)}, u32[]{:S(2)}, u32[]{:S(2)}) collective-permute-start(bf16[256,128]{1,0:T(8,128)(2,1)} %param.13), channel_id=1, source_target_pairs={{0,56},{8,0},{16,8},{24,16},{32,24},{40,32},{48,40},{56,48},{64,12... | collective-permute-start | bytes 196616 | tf_op jit(solution)/shard_map/ppermute | solution.py:18
  24.3 23.6 %copy-start.7 = (f32[640,256]{1,0:T(8,128)}, f32[640,256]{1,0:T(8,128)S(1)}, u32[]{:S(2)}) copy-start(f32[640,256]{1,0:T(8,128)S(1)} %get-tuple-element.90) | copy-start | bytes 1966084
  25.7 20.8 %all-to-all-start = ((bf16[8,80,512]{2,1,0:T(8,128)(2,1)}), bf16[8,80,512]{2,1,0:T(8,128)(2,1)S(1)}, u32[]{:S(2)}, u32[]{:S(2)}) async-start(bf16[8,80,512]{2,1,0:T(8,128)(2,1)} %bitcast.15), calls=%async_computation | async-start | bytes 1310720 | tf_op jit(solution)/shard_map/all_to_all | solution.py:228
  30.6 81.2 %all-gather.2.cloned.1.call-start = ((), (), s32[]{:S(2)}) async-start(), calls=%async_computation.6 | async-start | bytes 5898240 | tf_op jit(solution)/shard_map/all_gather | solution.py:238
  30.6 15.9 %collective-permute-start.5 = (bf16[3,256,128]{2,1,0:T(8,128)(2,1)S(1)}, bf16[3,256,128]{2,1,0:T(8,128)(2,1)S(1)}, u32[]{:S(2)}, u32[]{:S(2)}) collective-permute-start(bf16[3,256,128]{2,1,0:T(8,128)(2,1)S(1)} %pad_maximum_fusion.2), channel_id=1, source_target_pairs={{0,24},{8,32},{16,40},{24,48},{32,56},{40,0},{48,8},{56,16},{64,88... | collective-permute-start | bytes 589832 | tf_op jit(solution)/shard_map/ppermute | solution.py:18
  32.7 7.3 %collective-permute-start.6 = (bf16[2,256,128]{2,1,0:T(8,128)(2,1)S(1)}, bf16[2,256,128]{2,1,0:T(8,128)(2,1)S(1)}, u32[]{:S(2)}, u32[]{:S(2)}) collective-permute-start(bf16[2,256,128]{2,1,0:T(8,128)(2,1)S(1)} %slice.29), channel_id=1, source_target_pairs={{0,40},{8,48},{16,56},{24,0},{32,8},{40,16},{48,24},{56,32},{64,10... | collective-permute-start | bytes 393224 | tf_op jit(solution)/shard_map/ppermute | solution.py:18
  46.5 0.8 copy-start.11
  47.3 206.9 %reduce-scatter.2.cloned.1.call-start = ((), (), s32[]{:S(2)}) async-start(), calls=%async_computation.7 | async-start | bytes 5898240 | tf_op jit(solution)/shard_map/reduce_scatter | solution.py:299
  70.5 59.9 %collective-permute-start.10 = (bf16[640,1024]{1,0:T(8,128)(2,1)S(1)}, bf16[640,1024]{1,0:T(8,128)(2,1)S(1)}, u32[]{:S(2)}, u32[]{:S(2)}) collective-permute-start(bf16[640,1024]{1,0:T(8,128)(2,1)S(1)} %bitcast.142), channel_id=1, source_target_pairs={{0,64},{8,72},{16,80},{24,88},{32,96},{40,104},{48,112},{56,120},{... | collective-permute-start | bytes 3932168 | tf_op jit(solution)/shard_map/ppermute | solution.py:23
  71.1 59.2 %collective-permute-start.11 = (bf16[640,1024]{1,0:T(8,128)(2,1)S(1)}, bf16[640,1024]{1,0:T(8,128)(2,1)}, u32[]{:S(2)}, u32[]{:S(2)}) collective-permute-start(bf16[640,1024]{1,0:T(8,128)(2,1)S(1)} %bitcast.143), channel_id=1, source_target_pairs={{0,128},{8,136},{16,144},{24,152},{32,160},{40,168},{48,176},{56,1... | collective-permute-start | bytes 3932168 | tf_op jit(solution)/shard_map/ppermute | solution.py:23
  72.0 59.1 %collective-permute-start.12 = (bf16[640,1024]{1,0:T(8,128)(2,1)S(1)}, bf16[640,1024]{1,0:T(8,128)(2,1)}, u32[]{:S(2)}, u32[]{:S(2)}) collective-permute-start(bf16[640,1024]{1,0:T(8,128)(2,1)S(1)} %bitcast.144), channel_id=1, source_target_pairs={{0,192},{8,200},{16,208},{24,216},{32,224},{40,232},{48,240},{56,2... | collective-permute-start | bytes 3932168 | tf_op jit(solution)/shard_map/ppermute | solution.py:23
  125.6 1.1 copy-start.2
  130.4 1.1 copy-start
  144.9 0.7 copy-start.4
  145.6 0.7 copy-start.6
  146.4 4.9 %copy-start.1 = (bf16[640,1024]{1,0:T(8,128)(2,1)S(1)}, bf16[640,1024]{1,0:T(8,128)(2,1)}, u32[]{:S(2)}) copy-start(bf16[640,1024]{1,0:T(8,128)(2,1)} %copy-done) | copy-start | bytes 3932164
  146.4 31.6 %collective-permute-start.7 = (bf16[640,1024]{1,0:T(8,128)(2,1)}, bf16[640,1024]{1,0:T(8,128)(2,1)}, u32[]{:S(2)}, u32[]{:S(2)}) collective-permute-start(bf16[640,1024]{1,0:T(8,128)(2,1)} %get-tuple-element.39), channel_id=1, source_target_pairs={{0,64},{8,72},{16,80},{24,88},{32,96},{40,104},{48,112},{56,120},{... | collective-permute-start | bytes 3932168 | tf_op jit(solution)/shard_map/ppermute | solution.py:23
  146.5 60.3 %collective-permute-start.8 = (bf16[640,1024]{1,0:T(8,128)(2,1)}, bf16[640,1024]{1,0:T(8,128)(2,1)}, u32[]{:S(2)}, u32[]{:S(2)}) collective-permute-start(bf16[640,1024]{1,0:T(8,128)(2,1)} %get-tuple-element.40), channel_id=1, source_target_pairs={{0,128},{8,136},{16,144},{24,152},{32,160},{40,168},{48,176},{56,1... | collective-permute-start | bytes 3932168 | tf_op jit(solution)/shard_map/ppermute | solution.py:23
  150.0 56.8 %collective-permute-start.9 = (bf16[640,1024]{1,0:T(8,128)(2,1)}, bf16[640,1024]{1,0:T(8,128)(2,1)}, u32[]{:S(2)}, u32[]{:S(2)}) collective-permute-start(bf16[640,1024]{1,0:T(8,128)(2,1)} %get-tuple-element.41), channel_id=1, source_target_pairs={{0,192},{8,200},{16,208},{24,216},{32,224},{40,232},{48,240},{56,2... | collective-permute-start | bytes 3932168 | tf_op jit(solution)/shard_map/ppermute | solution.py:23
  151.2 1.0 copy-start.5
  152.2 54.6 %copy-start.3 = (bf16[640,1024]{1,0:T(8,128)(2,1)S(1)}, bf16[640,1024]{1,0:T(8,128)(2,1)}, u32[]{:S(2)}) copy-start(bf16[640,1024]{1,0:T(8,128)(2,1)} %copy-done.2) | copy-start | bytes 3932164
  211.1 33.7 %all-to-all-start.2 = ((bf16[8,80,1024]{2,1,0:T(8,128)(2,1)}), bf16[8,80,1024]{2,1,0:T(8,128)(2,1)S(1)}, u32[]{:S(2)}, u32[]{:S(2)}) async-start(bf16[8,80,1024]{2,1,0:T(8,128)(2,1)} %bitcast.30), calls=%async_computation.2 | async-start | bytes 2621440 | tf_op jit(solution)/shard_map/all_to_all | solution.py:228
  215.7 5.1 %collective-permute-start.20 = (f32[8,80]{1,0:T(8,128)S(1)}, f32[8,80]{1,0:T(8,128)S(1)}, u32[]{:S(2)}, u32[]{:S(2)}) collective-permute-start(f32[8,80]{1,0:T(8,128)S(1)} %reshape_squeeze.3), channel_id=1, source_target_pairs={{0,128},{8,136},{16,144},{24,152},{32,160},{40,168},{48,176},{56,1... | collective-permute-start | bytes 7688 | tf_op jit(solution)/shard_map/ppermute | solution.py:23
  220.8 4.8 %collective-permute-start.21 = (f32[8,80]{1,0:T(8,128)S(1)}, f32[8,80]{1,0:T(8,128)S(1)}, u32[]{:S(2)}, u32[]{:S(2)}) collective-permute-start(f32[8,80]{1,0:T(8,128)S(1)} %add.369), channel_id=1, source_target_pairs={{0,64},{8,72},{16,80},{24,88},{32,96},{40,104},{48,112},{56,120},{... | collective-permute-start | bytes 7688 | tf_op jit(solution)/shard_map/ppermute | solution.py:23
  225.6 8.1 %collective-permute-start.22 = (f32[8,80]{1,0:T(8,128)S(1)}, f32[8,80]{1,0:T(8,128)S(1)}, u32[]{:S(2)}, u32[]{:S(2)}) collective-permute-start(f32[8,80]{1,0:T(8,128)S(1)} %add.370), channel_id=1, source_target_pairs={{0,32},{8,40},{16,48},{24,56},{32,0},{40,8},{48,16},{56,24},{64,96... | collective-permute-start | bytes 7688 | tf_op jit(solution)/shard_map/ppermute | solution.py:18
  233.7 5.7 %collective-permute-start.23 = (f32[8,80]{1,0:T(8,128)S(1)}, f32[8,80]{1,0:T(8,128)S(1)}, u32[]{:S(2)}, u32[]{:S(2)}) collective-permute-start(f32[8,80]{1,0:T(8,128)S(1)} %add.371), channel_id=1, source_target_pairs={{0,16},{8,24},{16,32},{24,40},{32,48},{40,56},{48,0},{56,8},{64,80... | collective-permute-start | bytes 7688 | tf_op jit(solution)/shard_map/ppermute | solution.py:18
  239.5 4.8 %collective-permute-start.24 = (f32[8,80]{1,0:T(8,128)S(1)}, f32[8,80]{1,0:T(8,128)S(1)}, u32[]{:S(2)}, u32[]{:S(2)}) collective-permute-start(f32[8,80]{1,0:T(8,128)S(1)} %add.372), channel_id=1, source_target_pairs={{0,8},{8,16},{16,24},{24,32},{32,40},{40,48},{48,56},{56,0},{64,72... | collective-permute-start | bytes 7688 | tf_op jit(solution)/shard_map/ppermute | solution.py:18
  244.9 9.3 %all-to-all-start.4 = ((f32[8,1,80]{2,1,0:T(1,128)}), f32[8,1,80]{2,1,0:T(1,128)S(1)}, u32[]{:S(2)}, u32[]{:S(2)}) async-start(f32[8,1,80]{2,1,0:T(1,128)} %bitcast.58), calls=%async_computation.5 | async-start | bytes 8192 | tf_op jit(solution)/shard_map/all_to_all | solution.py:338
  249.7 1.1 copy-start.10
  253.2 1.0 copy-start.9
  254.2 10.1 %copy-start.14 = (f32[256,2]{0,1:T(2,128)S(1)}, f32[256,2]{0,1:T(2,128)}, u32[]{:S(2)}) copy-start(f32[256,2]{0,1:T(2,128)} %param.9) | copy-start | bytes 6148
  254.2 27.6 %all-to-all-start.3 = ((bf16[8,80,512]{2,1,0:T(8,128)(2,1)}), bf16[8,80,512]{2,1,0:T(8,128)(2,1)S(1)}, u32[]{:S(2)}, u32[]{:S(2)}) async-start(bf16[8,80,512]{2,1,0:T(8,128)(2,1)} %bitcast.160), calls=%async_computation.4 | async-start | bytes 1310720 | tf_op jit(solution)/shard_map/all_to_all | solution.py:228
  259.1 18.4 %collective-permute-start.13 = (bf16[3,256,128]{2,1,0:T(8,128)(2,1)S(1)}, bf16[3,256,128]{2,1,0:T(8,128)(2,1)S(1)}, u32[]{:S(2)}, u32[]{:S(2)}) collective-permute-start(bf16[3,256,128]{2,1,0:T(8,128)(2,1)S(1)} %pad_maximum_fusion.3), channel_id=1, source_target_pairs={{0,24},{8,32},{16,40},{24,48},{32,56},{40,0},{48,8},{56,16},{64,88... | collective-permute-start | bytes 589832 | tf_op jit(solution)/shard_map/ppermute | solution.py:18
  262.2 7.4 %collective-permute-start.14 = (bf16[2,256,128]{2,1,0:T(8,128)(2,1)S(1)}, bf16[2,256,128]{2,1,0:T(8,128)(2,1)S(1)}, u32[]{:S(2)}, u32[]{:S(2)}) collective-permute-start(bf16[2,256,128]{2,1,0:T(8,128)(2,1)S(1)} %pad_maximum_fusion.4), channel_id=1, source_target_pairs={{0,40},{8,48},{16,56},{24,0},{32,8},{40,16},{48,24},{56,32},{64,10... | collective-permute-start | bytes 393224 | tf_op jit(solution)/shard_map/ppermute | solution.py:18
  269.6 12.6 %copy-start.8 = (f32[640,256]{1,0:T(8,128)S(1)}, f32[640,256]{1,0:T(8,128)}, u32[]{:S(2)}) copy-start(f32[640,256]{1,0:T(8,128)} %copy-done.7) | copy-start | bytes 1966084
  278.5 8.3 %collective-permute-start.15 = (bf16[256,128]{1,0:T(8,128)(2,1)S(1)}, bf16[256,128]{1,0:T(8,128)(2,1)S(1)}, u32[]{:S(2)}, u32[]{:S(2)}) collective-permute-start(bf16[256,128]{1,0:T(8,128)(2,1)S(1)} %get-tuple-element.93), channel_id=1, source_target_pairs={{0,8},{8,16},{16,24},{24,32},{32,40},{40,48},{48,56},{56,0},{64,72... | collective-permute-start | bytes 196616 | tf_op jit(solution)/shard_map/ppermute | solution.py:18
  278.9 7.9 %collective-permute-start.16 = (bf16[256,128]{1,0:T(8,128)(2,1)S(1)}, bf16[256,128]{1,0:T(8,128)(2,1)S(1)}, u32[]{:S(2)}, u32[]{:S(2)}) collective-permute-start(bf16[256,128]{1,0:T(8,128)(2,1)S(1)} %get-tuple-element.94), channel_id=1, source_target_pairs={{0,56},{8,0},{16,8},{24,16},{32,24},{40,32},{48,40},{56,48},{64,12... | collective-permute-start | bytes 196616 | tf_op jit(solution)/shard_map/ppermute | solution.py:18
  283.5 6.3 %collective-permute-start.17 = (bf16[256,128]{1,0:T(8,128)(2,1)S(1)}, bf16[256,128]{1,0:T(8,128)(2,1)S(1)}, u32[]{:S(2)}, u32[]{:S(2)}) collective-permute-start(bf16[256,128]{1,0:T(8,128)(2,1)S(1)} %get-tuple-element.100), channel_id=1, source_target_pairs={{0,64},{8,72},{16,80},{24,88},{32,96},{40,104},{48,112},{56,120},{... | collective-permute-start | bytes 196616 | tf_op jit(solution)/shard_map/ppermute | solution.py:23
  283.6 6.2 %collective-permute-start.18 = (bf16[256,128]{1,0:T(8,128)(2,1)S(1)}, bf16[256,128]{1,0:T(8,128)(2,1)S(1)}, u32[]{:S(2)}, u32[]{:S(2)}) collective-permute-start(bf16[256,128]{1,0:T(8,128)(2,1)S(1)} %get-tuple-element.102), channel_id=1, source_target_pairs={{0,128},{8,136},{16,144},{24,152},{32,160},{40,168},{48,176},{56,1... | collective-permute-start | bytes 196616 | tf_op jit(solution)/shard_map/ppermute | solution.py:23
  286.0 4.6 %collective-permute-start.19 = (bf16[256,128]{1,0:T(8,128)(2,1)S(1)}, bf16[256,128]{1,0:T(8,128)(2,1)S(1)}, u32[]{:S(2)}, u32[]{:S(2)}) collective-permute-start(bf16[256,128]{1,0:T(8,128)(2,1)S(1)} %get-tuple-element.101), channel_id=1, source_target_pairs={{0,192},{8,200},{16,208},{24,216},{32,224},{40,232},{48,240},{56,2... | collective-permute-start | bytes 196616 | tf_op jit(solution)/shard_map/ppermute | solution.py:23
Sparse Core Ops, SparseCore 0:
  47.5 64.2 all-gather.1
  146.5 65.0 reduce-scatter.1
